TPU v7x, 32 devices: a whole 2x2x4 slice. The times are simulated.
32 devices in a mesh: groups: 2 (over y), section: 4 (over z), replica: 4 (over x, core).
Axes of the slice: x: 2, y: 2, z: 4, core: 2. Of those that a mesh axis runs over, the one named last changes fastest.
Arguments:
- section_inputs: bfloat16 [8, 4, 2, 16, 16, 256], P(('groups', 'replica'), 'section'), parts along dimension 0, may hold values from -6 to 6
- cotangent: bfloat16 [8, 2, 16, 16, 256], P(('groups', 'replica')), parts along dimension 0, may hold values from -6 to 6
- crop_rows: int32 [8, 2], P(('groups', 'replica')), parts along dimension 0, may hold values from 0 to 705
- drift: bfloat16 [8, 4, 9, 256, 256], P(('groups', 'replica'), 'section'), parts along dimension 0, may hold values from -6 to 6
- params: float32 [8, 9, 256, 256], P(('groups', 'section')), parts along dimension 0, may hold values from -6 to 6
- momentum: float32 [8, 9, 256, 256], P(('groups', 'section'), None, 'replica'), parts along dimension 0, may hold values from -4 to 4
Outputs:
- new_params: float32 [8, 9, 256, 256], P(('groups', 'section')), parts along dimension 0
- new_momentum: float32 [8, 9, 256, 256], P(('groups', 'section'), None, 'replica'), parts along dimension 0
There are 2 independent parts, one for each index of `groups`. A program takes and returns all parts, laid end to end along the dimension named above; each array names one. Nothing has to cross between parts.
All inputs are finite; a program needn't handle non-finite values.
Results may differ from a plain program's by a relative error of at most 0.0075.
Values may be sent and summed in bfloat16 or wider, within the bound.
No kernel may reach another device: no remote copies, remote signals or barrier semaphores. Data moves between devices by JAX's collectives and lax.ppermute only.
A program may use at most 64 MiB of HBM per device.

v0:
```python
import math
import jax
import jax.numpy as jnp
from jax import lax
from jax.sharding import PartitionSpec as P

LATS = 721


def from_behind(x, axis, by):
    devices = lax.axis_size(axis)
    pairs = [(i, i + by) for i in range(devices) if 0 <= i + by < devices]
    return lax.ppermute(x, axis, pairs)


def lat_weight(first_row, count):
    rows = jnp.arange(count, dtype=jnp.float32) + first_row.astype(jnp.float32)
    middle = (LATS - 1) / 2.0
    every = jnp.arange(LATS, dtype=jnp.float32)
    norm_value = jnp.mean(jnp.cos(math.pi * (every - middle) / (LATS - 1)))
    return jnp.cos(math.pi * (rows - middle) / (LATS - 1)) / norm_value


def backward(inputs, out_grad, weights):
    rows, cols, width = inputs.shape
    scale = (9.0 * width) ** (-0.5)
    padded = jnp.pad(inputs, ((1, 1), (1, 1), (0, 0)))
    taps = jnp.stack([padded[a : a + rows, b : b + cols] for a in range(3) for b in range(3)])
    pre = jnp.einsum("krcd,kde->rce", taps, weights, preferred_element_type=jnp.float32) * scale
    tangent = jnp.tanh(pre)
    local = (out_grad.astype(jnp.float32) * (1.0 - tangent * tangent)).astype(jnp.bfloat16)
    grad = jnp.einsum("krcd,rce->kde", taps, local, preferred_element_type=jnp.float32) * scale
    back = jnp.einsum("rce,kde->krcd", local, weights, preferred_element_type=jnp.float32)
    accum = jnp.zeros((rows + 2, cols + 2, width), jnp.float32)
    for a in range(3):
        for b in range(3):
            accum = accum.at[a : a + rows, b : b + cols].add(back[3 * a + b])
    in_grad = (out_grad.astype(jnp.float32) + scale * accum[1 : rows + 1, 1 : cols + 1]).astype(
        jnp.bfloat16
    )
    return (grad, in_grad)


def per_device(section_inputs, cotangent, crop_rows, drift, params, momentum):
    section = lax.axis_index("section")
    sections = lax.axis_size("section")
    inputs_here = section_inputs[0, 0]
    cot_here = cotangent[0]
    crops_here = crop_rows[0]
    micro = inputs_here.shape[0]
    rows, cols, width = inputs_here.shape[1:]
    weights_bf = params[0].astype(jnp.bfloat16)

    def tick(step, carry):
        incoming, grad_total = carry
        micro_index = step - (sections - 1 - section)
        valid = jnp.logical_and(micro_index >= 0, micro_index < micro)
        chosen = jnp.clip(micro_index, 0, micro - 1)
        inputs_now = lax.dynamic_index_in_dim(inputs_here, chosen, 0, keepdims=False)
        cot_now = lax.dynamic_index_in_dim(cot_here, chosen, 0, keepdims=False)
        first_row = lax.dynamic_index_in_dim(crops_here, chosen, 0, keepdims=False)
        top_grad = (
            cot_now.astype(jnp.float32) * lat_weight(first_row, rows)[:, None, None]
        ).astype(jnp.bfloat16)
        out_grad = jnp.where(section == sections - 1, top_grad, incoming)
        contrib, in_grad = backward(inputs_now, out_grad, weights_bf)
        grad_total = grad_total + jnp.where(valid, contrib, jnp.zeros_like(contrib))
        passed = from_behind(in_grad, "section", -1)
        return (passed, grad_total)

    start = (
        jnp.zeros((rows, cols, width), jnp.bfloat16),
        jnp.zeros((9, width, width), jnp.float32),
    )
    unused, grad_total = lax.fori_loop(0, sections + micro - 1, tick, start)
    delta_bf = (drift[0, 0].astype(jnp.float32) + 0.5 * grad_total).astype(jnp.bfloat16)
    delta_bf = lax.optimization_barrier(delta_bf)
    delta = delta_bf.astype(jnp.float32)
    replicas = lax.axis_size("replica")
    here = lax.axis_index("replica")
    share_rows = width // replicas
    mean_delta = lax.psum(delta.astype(jnp.bfloat16), "replica").astype(jnp.float32) / replicas
    mom_whole = lax.all_gather(momentum[0], "replica", axis=1, tiled=True)
    mom_next = 0.9 * mom_whole + mean_delta
    new_params = params[0] - 0.7 * (mean_delta + 0.9 * mom_next)
    new_momentum = lax.dynamic_slice_in_dim(mom_next, here * share_rows, share_rows, 1)
    return (new_params[None], new_momentum[None])


def solution(mesh):
    placed = (
        P(("groups", "replica"), "section", None, None, None, None),
        P(("groups", "replica"), None, None, None, None),
        P(("groups", "replica"), None),
        P(("groups", "replica"), "section", None, None, None),
        P(("groups", "section"), None, None, None),
        P(("groups", "section"), None, "replica", None),
    )
    return jax.shard_map(
        per_device,
        mesh=mesh,
        in_specs=placed,
        out_specs=(
            P(("groups", "section"), None, None, None),
            P(("groups", "section"), None, "replica", None),
        ),
        check_vma=False,
    )
```

profile of v0, /device:TPU:0, one launch (start us, length us, event | category | flops | bytes accessed | tf_op | source)
XLA Modules:
  0.0 208.0 jit_solution(15496415123760340458)
XLA Ops:
  7.3 1.8 bitcast_convert_fusion
  9.1 119.2 %while.28 = (s32[]{:T(128)}, bf16[16,16,256]{2,1,0:T(8,128)(2,1)S(1)}, f32[9,256,256]{2,1,0:T(8,128)}, pred[]{:T(512)}, s32[]{:T(128)}, /*index=5*/bf16[2,16,16,...) while((s32[]{:T(128)}, ...), condition=%wide.region_3.4_spmd.clone, body=%wide.region_0.3_spmd.clone.sunk | while | flops 910100672 | bytes 44110644 | solution.py:75
  12.6 1.4 fusion.102
  17.2 1.6 scatter-add.71
  19.5 1.9 add_select_fusion.2
  21.4 1.6 scatter-add.72
  27.2 3.4 %fusion.113 = f32[9,256,256]{2,1,0:T(8,128)} fusion(f32[9,256,256]{2,1,0:T(8,128)} %get-tuple-element.608, bf16[9,16,16,256]{3,2,0,1:T(8,128)(2,1)} %copy-done.7, pred[]{:T(512)S(6)} %compare.180, pred[]{:T(512)S(6)} %and.113, bf16[16,16,256]{2,1,0:T(8,128)(2,1)} %copy-done.6), kind=kOutput, calls=%fused_computation.2.clone.1 | convolution fusion | flops 304349184 | bytes 6029314 | tf_op jit(solution)/shard_map/while/body/eval_jaxpr/krcd,rce->kde/dot_general | solution.py:32
  30.6 3.7 %collective-permute-done = bf16[16,16,256]{2,1,0:T(8,128)(2,1)S(1)} collective-permute-done((bf16[16,16,256]{2,1,0:T(8,128)(2,1)S(1)}, bf16[16,16,256]{2,1,0:T(8,128)(2,1)S(1)}, u32[]{:S(2)}, u32[]{:S(2)}) %collective-permute-start) | collective-permute-done | bytes 131104 | tf_op jit(solution)/shard_map/while/body/eval_jaxpr/ppermute | solution.py:13
  37.7 1.4 fusion.102
  42.3 1.6 scatter-add.71
  44.6 1.9 add_select_fusion.2
  46.5 1.6 scatter-add.72
  52.3 4.2 %fusion.113 = f32[9,256,256]{2,1,0:T(8,128)} fusion(f32[9,256,256]{2,1,0:T(8,128)} %get-tuple-element.608, bf16[9,16,16,256]{3,2,0,1:T(8,128)(2,1)} %copy-done.7, pred[]{:T(512)S(6)} %compare.180, pred[]{:T(512)S(6)} %and.113, bf16[16,16,256]{2,1,0:T(8,128)(2,1)} %copy-done.6), kind=kOutput, calls=%fused_computation.2.clone.1 | convolution fusion | flops 304349184 | bytes 6029314 | tf_op jit(solution)/shard_map/while/body/eval_jaxpr/krcd,rce->kde/dot_general | solution.py:32
  61.2 1.4 fusion.102
  65.8 1.6 scatter-add.71
  68.2 1.9 add_select_fusion.2
  70.1 1.6 scatter-add.72
  75.8 4.2 %fusion.113 = f32[9,256,256]{2,1,0:T(8,128)} fusion(f32[9,256,256]{2,1,0:T(8,128)} %get-tuple-element.608, bf16[9,16,16,256]{3,2,0,1:T(8,128)(2,1)} %copy-done.7, pred[]{:T(512)S(6)} %compare.180, pred[]{:T(512)S(6)} %and.113, bf16[16,16,256]{2,1,0:T(8,128)(2,1)} %copy-done.6), kind=kOutput, calls=%fused_computation.2.clone.1 | convolution fusion | flops 304349184 | bytes 6029314 | tf_op jit(solution)/shard_map/while/body/eval_jaxpr/krcd,rce->kde/dot_general | solution.py:32
  84.7 1.4 fusion.102
  89.3 1.6 scatter-add.71
  91.7 1.9 add_select_fusion.2
  93.6 1.6 scatter-add.72
  99.3 4.2 %fusion.113 = f32[9,256,256]{2,1,0:T(8,128)} fusion(f32[9,256,256]{2,1,0:T(8,128)} %get-tuple-element.608, bf16[9,16,16,256]{3,2,0,1:T(8,128)(2,1)} %copy-done.7, pred[]{:T(512)S(6)} %compare.180, pred[]{:T(512)S(6)} %and.113, bf16[16,16,256]{2,1,0:T(8,128)(2,1)} %copy-done.6), kind=kOutput, calls=%fused_computation.2.clone.1 | convolution fusion | flops 304349184 | bytes 6029314 | tf_op jit(solution)/shard_map/while/body/eval_jaxpr/krcd,rce->kde/dot_general | solution.py:32
  108.2 1.4 fusion.102
  112.9 1.6 scatter-add.71
  115.2 1.9 add_select_fusion.2
  117.1 1.6 scatter-add.72
  122.9 4.2 %fusion.113 = f32[9,256,256]{2,1,0:T(8,128)} fusion(f32[9,256,256]{2,1,0:T(8,128)} %get-tuple-element.608, bf16[9,16,16,256]{3,2,0,1:T(8,128)(2,1)} %copy-done.7, pred[]{:T(512)S(6)} %compare.180, pred[]{:T(512)S(6)} %and.113, bf16[16,16,256]{2,1,0:T(8,128)(2,1)} %copy-done.6), kind=kOutput, calls=%fused_computation.2.clone.1 | convolution fusion | flops 304349184 | bytes 6029314 | tf_op jit(solution)/shard_map/while/body/eval_jaxpr/krcd,rce->kde/dot_general | solution.py:32
  128.4 3.5 %fusion.56 = bf16[9,256,256]{2,1,0:T(8,128)(2,1)} fusion(f32[9,256,256]{2,1,0:T(8,128)} %get-tuple-element.472, bf16[1,1,9,256,256]{4,3,2,1,0:T(8,128)(2,1)} %param.29), kind=kLoop, calls=%fused_computation.72 | loop fusion | flops 2359296 | bytes 4718592 | tf_op jit(solution)/shard_map/convert_element_type | solution.py:76
  132.6 37.8 %all-reduce.4.cloned.1.call-done = bf16[9,256,256]{2,1,0:T(8,128)(2,1)} async-done(((bf16[9,256,256]{2,1,0:T(8,128)(2,1)}), bf16[9,256,256]{2,1,0:T(8,128)(2,1)}) %all-reduce.4.cloned.1.call-update) | async-done | bytes 1179664 | tf_op jit(solution)/shard_map/psum | solution.py:82
  170.5 25.8 %all-gather.3.cloned.1.call-done = f32[1,9,256,256]{3,2,1,0:T(8,128)} async-done(((f32[1,9,64,256]{3,2,1,0:T(8,128)}), f32[1,9,256,256]{3,2,1,0:T(8,128)}) %all-gather.3.cloned.1.call-update) | async-done | bytes 2359312 | tf_op jit(solution)/shard_map/all_gather | solution.py:83
  196.3 4.0 %bitcast_add_fusion = (f32[9,256,256]{2,1,0:T(8,128)S(1)}, f32[1,9,256,256]{3,2,1,0:T(8,128)}) fusion(f32[1,9,256,256]{3,2,1,0:T(8,128)} %all-gather.3.cloned.1.call-done, bf16[9,256,256]{2,1,0:T(8,128)(2,1)} %all-reduce.4.cloned.1.call-done, f32[1,9,256,256]{3,2,1,0:T(8,128)S(1)} %copy-done.4), kind=kLoop, calls=%fused_computation.73 | loop fusion | flops 4718592 | bytes 10616832 | tf_op jit(solution)/shard_map/add | solution.py:84
  (260 shorter events, 56.6 us)
Async XLA Ops:
  7.2 163.3 %all-reduce.4.cloned.1.call-start = ((), (), s32[]{:S(2)}) async-start(), calls=%async_computation | async-start | bytes 2359296 | tf_op jit(solution)/shard_map/psum | solution.py:82
  9.2 3.4 %copy-start.2 = (bf16[2,16,16,256]{3,2,0,1:T(8,128)(2,1)}, bf16[2,16,16,256]{3,2,0,1:T(8,128)(2,1)S(1)}, u32[]{:S(2)}) copy-start(bf16[2,16,16,256]{3,2,0,1:T(8,128)(2,1)S(1)} %get-tuple-element.629) | copy-start | bytes 786436 | tf_op jit(solution)/shard_map/while
  9.2 3.4 %copy-start.5 = (bf16[16,16,256]{2,1,0:T(8,128)(2,1)}, bf16[16,16,256]{2,1,0:T(8,128)(2,1)S(1)}, u32[]{:S(2)}) copy-start(bf16[16,16,256]{2,1,0:T(8,128)(2,1)S(1)} %get-tuple-element.607) | copy-start | bytes 393220 | tf_op jit(solution)/shard_map/while
  9.2 4.8 %copy-start = (bf16[9,256,256]{2,1,0:T(8,128)(2,1)}, bf16[9,256,256]{2,1,0:T(8,128)(2,1)S(1)}, u32[]{:S(2)}) copy-start(bf16[9,256,256]{2,1,0:T(8,128)(2,1)S(1)} %get-tuple-element.630) | copy-start | bytes 3538948 | tf_op jit(solution)/shard_map/while
  25.8 8.4 %collective-permute-start = (bf16[16,16,256]{2,1,0:T(8,128)(2,1)S(1)}, bf16[16,16,256]{2,1,0:T(8,128)(2,1)S(1)}, u32[]{:S(2)}, u32[]{:S(2)}) collective-permute-start(bf16[16,16,256]{2,1,0:T(8,128)(2,1)S(1)} %fusion.112), channel_id=1, source_target_pairs={{4,0},{8,4},{12,8},{5,1},{9,5},{13,9},{6,2},{10,6},{14,10},{7,3},{... | collective-permute-start | bytes 393224 | tf_op jit(solution)/shard_map/while/body/eval_jaxpr/ppermute | solution.py:13
  27.2 7.1 %copy-start.1 = (bf16[9,256,256]{2,1,0:T(8,128)(2,1)S(1)}, bf16[9,256,256]{2,1,0:T(8,128)(2,1)}, u32[]{:S(2)}) copy-start(bf16[9,256,256]{2,1,0:T(8,128)(2,1)} %copy-done) | copy-start | bytes 3538948 | tf_op jit(solution)/shard_map/while
  27.2 7.1 %copy-start.3 = (bf16[2,16,16,256]{3,2,0,1:T(8,128)(2,1)S(1)}, bf16[2,16,16,256]{3,2,0,1:T(8,128)(2,1)}, u32[]{:S(2)}) copy-start(bf16[2,16,16,256]{3,2,0,1:T(8,128)(2,1)} %copy-done.2) | copy-start | bytes 786436 | tf_op jit(solution)/shard_map/while
  34.3 3.4 %copy-start.2 = (bf16[2,16,16,256]{3,2,0,1:T(8,128)(2,1)}, bf16[2,16,16,256]{3,2,0,1:T(8,128)(2,1)S(1)}, u32[]{:S(2)}) copy-start(bf16[2,16,16,256]{3,2,0,1:T(8,128)(2,1)S(1)} %get-tuple-element.629) | copy-start | bytes 786436 | tf_op jit(solution)/shard_map/while
  34.3 3.4 %copy-start.5 = (bf16[16,16,256]{2,1,0:T(8,128)(2,1)}, bf16[16,16,256]{2,1,0:T(8,128)(2,1)S(1)}, u32[]{:S(2)}) copy-start(bf16[16,16,256]{2,1,0:T(8,128)(2,1)S(1)} %get-tuple-element.607) | copy-start | bytes 393220 | tf_op jit(solution)/shard_map/while
  34.3 4.8 %copy-start = (bf16[9,256,256]{2,1,0:T(8,128)(2,1)}, bf16[9,256,256]{2,1,0:T(8,128)(2,1)S(1)}, u32[]{:S(2)}) copy-start(bf16[9,256,256]{2,1,0:T(8,128)(2,1)S(1)} %get-tuple-element.630) | copy-start | bytes 3538948 | tf_op jit(solution)/shard_map/while
  50.9 6.9 %collective-permute-start = (bf16[16,16,256]{2,1,0:T(8,128)(2,1)S(1)}, bf16[16,16,256]{2,1,0:T(8,128)(2,1)S(1)}, u32[]{:S(2)}, u32[]{:S(2)}) collective-permute-start(bf16[16,16,256]{2,1,0:T(8,128)(2,1)S(1)} %fusion.112), channel_id=1, source_target_pairs={{4,0},{8,4},{12,8},{5,1},{9,5},{13,9},{6,2},{10,6},{14,10},{7,3},{... | collective-permute-start | bytes 393224 | tf_op jit(solution)/shard_map/while/body/eval_jaxpr/ppermute | solution.py:13
  52.2 5.6 %copy-start.1 = (bf16[9,256,256]{2,1,0:T(8,128)(2,1)S(1)}, bf16[9,256,256]{2,1,0:T(8,128)(2,1)}, u32[]{:S(2)}) copy-start(bf16[9,256,256]{2,1,0:T(8,128)(2,1)} %copy-done) | copy-start | bytes 3538948 | tf_op jit(solution)/shard_map/while
  52.3 5.5 %copy-start.3 = (bf16[2,16,16,256]{3,2,0,1:T(8,128)(2,1)S(1)}, bf16[2,16,16,256]{3,2,0,1:T(8,128)(2,1)}, u32[]{:S(2)}) copy-start(bf16[2,16,16,256]{3,2,0,1:T(8,128)(2,1)} %copy-done.2) | copy-start | bytes 786436 | tf_op jit(solution)/shard_map/while
  57.8 3.4 %copy-start.2 = (bf16[2,16,16,256]{3,2,0,1:T(8,128)(2,1)}, bf16[2,16,16,256]{3,2,0,1:T(8,128)(2,1)S(1)}, u32[]{:S(2)}) copy-start(bf16[2,16,16,256]{3,2,0,1:T(8,128)(2,1)S(1)} %get-tuple-element.629) | copy-start | bytes 786436 | tf_op jit(solution)/shard_map/while
  57.8 3.4 %copy-start.5 = (bf16[16,16,256]{2,1,0:T(8,128)(2,1)}, bf16[16,16,256]{2,1,0:T(8,128)(2,1)S(1)}, u32[]{:S(2)}) copy-start(bf16[16,16,256]{2,1,0:T(8,128)(2,1)S(1)} %get-tuple-element.607) | copy-start | bytes 393220 | tf_op jit(solution)/shard_map/while
  57.8 4.8 %copy-start = (bf16[9,256,256]{2,1,0:T(8,128)(2,1)}, bf16[9,256,256]{2,1,0:T(8,128)(2,1)S(1)}, u32[]{:S(2)}) copy-start(bf16[9,256,256]{2,1,0:T(8,128)(2,1)S(1)} %get-tuple-element.630) | copy-start | bytes 3538948 | tf_op jit(solution)/shard_map/while
  74.5 6.9 %collective-permute-start = (bf16[16,16,256]{2,1,0:T(8,128)(2,1)S(1)}, bf16[16,16,256]{2,1,0:T(8,128)(2,1)S(1)}, u32[]{:S(2)}, u32[]{:S(2)}) collective-permute-start(bf16[16,16,256]{2,1,0:T(8,128)(2,1)S(1)} %fusion.112), channel_id=1, source_target_pairs={{4,0},{8,4},{12,8},{5,1},{9,5},{13,9},{6,2},{10,6},{14,10},{7,3},{... | collective-permute-start | bytes 393224 | tf_op jit(solution)/shard_map/while/body/eval_jaxpr/ppermute | solution.py:13
  75.8 5.6 %copy-start.1 = (bf16[9,256,256]{2,1,0:T(8,128)(2,1)S(1)}, bf16[9,256,256]{2,1,0:T(8,128)(2,1)}, u32[]{:S(2)}) copy-start(bf16[9,256,256]{2,1,0:T(8,128)(2,1)} %copy-done) | copy-start | bytes 3538948 | tf_op jit(solution)/shard_map/while
  75.8 5.5 %copy-start.3 = (bf16[2,16,16,256]{3,2,0,1:T(8,128)(2,1)S(1)}, bf16[2,16,16,256]{3,2,0,1:T(8,128)(2,1)}, u32[]{:S(2)}) copy-start(bf16[2,16,16,256]{3,2,0,1:T(8,128)(2,1)} %copy-done.2) | copy-start | bytes 786436 | tf_op jit(solution)/shard_map/while
  81.3 3.4 %copy-start.2 = (bf16[2,16,16,256]{3,2,0,1:T(8,128)(2,1)}, bf16[2,16,16,256]{3,2,0,1:T(8,128)(2,1)S(1)}, u32[]{:S(2)}) copy-start(bf16[2,16,16,256]{3,2,0,1:T(8,128)(2,1)S(1)} %get-tuple-element.629) | copy-start | bytes 786436 | tf_op jit(solution)/shard_map/while
  81.3 3.4 %copy-start.5 = (bf16[16,16,256]{2,1,0:T(8,128)(2,1)}, bf16[16,16,256]{2,1,0:T(8,128)(2,1)S(1)}, u32[]{:S(2)}) copy-start(bf16[16,16,256]{2,1,0:T(8,128)(2,1)S(1)} %get-tuple-element.607) | copy-start | bytes 393220 | tf_op jit(solution)/shard_map/while
  81.3 4.8 %copy-start = (bf16[9,256,256]{2,1,0:T(8,128)(2,1)}, bf16[9,256,256]{2,1,0:T(8,128)(2,1)S(1)}, u32[]{:S(2)}) copy-start(bf16[9,256,256]{2,1,0:T(8,128)(2,1)S(1)} %get-tuple-element.630) | copy-start | bytes 3538948 | tf_op jit(solution)/shard_map/while
  98.0 6.9 %collective-permute-start = (bf16[16,16,256]{2,1,0:T(8,128)(2,1)S(1)}, bf16[16,16,256]{2,1,0:T(8,128)(2,1)S(1)}, u32[]{:S(2)}, u32[]{:S(2)}) collective-permute-start(bf16[16,16,256]{2,1,0:T(8,128)(2,1)S(1)} %fusion.112), channel_id=1, source_target_pairs={{4,0},{8,4},{12,8},{5,1},{9,5},{13,9},{6,2},{10,6},{14,10},{7,3},{... | collective-permute-start | bytes 393224 | tf_op jit(solution)/shard_map/while/body/eval_jaxpr/ppermute | solution.py:13
  99.3 5.6 %copy-start.1 = (bf16[9,256,256]{2,1,0:T(8,128)(2,1)S(1)}, bf16[9,256,256]{2,1,0:T(8,128)(2,1)}, u32[]{:S(2)}) copy-start(bf16[9,256,256]{2,1,0:T(8,128)(2,1)} %copy-done) | copy-start | bytes 3538948 | tf_op jit(solution)/shard_map/while
  99.3 5.5 %copy-start.3 = (bf16[2,16,16,256]{3,2,0,1:T(8,128)(2,1)S(1)}, bf16[2,16,16,256]{3,2,0,1:T(8,128)(2,1)}, u32[]{:S(2)}) copy-start(bf16[2,16,16,256]{3,2,0,1:T(8,128)(2,1)} %copy-done.2) | copy-start | bytes 786436 | tf_op jit(solution)/shard_map/while
  104.9 3.4 %copy-start.5 = (bf16[16,16,256]{2,1,0:T(8,128)(2,1)}, bf16[16,16,256]{2,1,0:T(8,128)(2,1)S(1)}, u32[]{:S(2)}) copy-start(bf16[16,16,256]{2,1,0:T(8,128)(2,1)S(1)} %get-tuple-element.607) | copy-start | bytes 393220 | tf_op jit(solution)/shard_map/while
  104.9 4.8 %copy-start = (bf16[9,256,256]{2,1,0:T(8,128)(2,1)}, bf16[9,256,256]{2,1,0:T(8,128)(2,1)S(1)}, u32[]{:S(2)}) copy-start(bf16[9,256,256]{2,1,0:T(8,128)(2,1)S(1)} %get-tuple-element.630) | copy-start | bytes 3538948 | tf_op jit(solution)/shard_map/while
  121.5 6.9 %collective-permute-start = (bf16[16,16,256]{2,1,0:T(8,128)(2,1)S(1)}, bf16[16,16,256]{2,1,0:T(8,128)(2,1)S(1)}, u32[]{:S(2)}, u32[]{:S(2)}) collective-permute-start(bf16[16,16,256]{2,1,0:T(8,128)(2,1)S(1)} %fusion.112), channel_id=1, source_target_pairs={{4,0},{8,4},{12,8},{5,1},{9,5},{13,9},{6,2},{10,6},{14,10},{7,3},{... | collective-permute-start | bytes 393224 | tf_op jit(solution)/shard_map/while/body/eval_jaxpr/ppermute | solution.py:13
  122.8 5.6 %copy-start.1 = (bf16[9,256,256]{2,1,0:T(8,128)(2,1)S(1)}, bf16[9,256,256]{2,1,0:T(8,128)(2,1)}, u32[]{:S(2)}) copy-start(bf16[9,256,256]{2,1,0:T(8,128)(2,1)} %copy-done) | copy-start | bytes 3538948 | tf_op jit(solution)/shard_map/while
  122.9 5.5 %copy-start.3 = (bf16[2,16,16,256]{3,2,0,1:T(8,128)(2,1)S(1)}, bf16[2,16,16,256]{3,2,0,1:T(8,128)(2,1)}, u32[]{:S(2)}) copy-start(bf16[2,16,16,256]{3,2,0,1:T(8,128)(2,1)} %copy-done.2) | copy-start | bytes 786436 | tf_op jit(solution)/shard_map/while
  128.4 67.9 %copy-start.4 = (f32[1,9,256,256]{3,2,1,0:T(8,128)S(1)}, f32[1,9,256,256]{3,2,1,0:T(8,128)}, u32[]{:S(2)}) copy-start(f32[1,9,256,256]{3,2,1,0:T(8,128)} %param.30) | copy-start | bytes 7077892
  131.9 64.4 %all-gather.3.cloned.1.call-start = ((), (), s32[]{:S(2)}) async-start(), calls=%async_computation.1 | async-start | bytes 2949120 | tf_op jit(solution)/shard_map/all_gather | solution.py:83
  (14 other events, 29.3 us)
Sparse Core Ops, SparseCore 0:
  132.0 38.4 all-reduce.3
  172.0 24.1 all-gather.2
where the time goes:
time: 209 us; the launch traced here: 208 us
  waiting for transfers between devices  73.4 us (35%)
  other arithmetic  40.8 us (20%)
  local copies, waits for them, and re-layouts  35.3 us (17%)
  matrix products  29.7 us (14%)
  between operations  14.1 us (7%)
  loops' own time  8.19 us (4%)
  starting transfers between devices  6.54 us (3%)
    psum x1, waiting for transfers between devices, per_device(): lax.psum(delta.astype(jnp.bfloat16), 'replica').astype(jnp.float32)  37.8 us
    all_gather x1, waiting for transfers between devices, per_device(): mom_whole = lax.all_gather(momentum[0], 'replica', axis=1, tiled=True)  25.8 us
    scatter-add x35, local copies, waits for them, and re-layouts, backward(): accum = accum.at[a:a + rows, b:b + cols].add(back[3 * a + b])  22.7 us
    dot_general x5, matrix products, backward(): jnp.einsum('krcd,rce->kde', taps, local, preferred_element_type=jnp.float32)  20.2 us
    another operation x15, other arithmetic  13.3 us
    ppermute x5, waiting for transfers between devices, from_behind(): return lax.ppermute(x, axis, pairs)  9.02 us
    another operation x1, loops' own time, per_device(): unused, grad_total = lax.fori_loop(0, sections + micro - 1, tick, start)  8.19 us
    add x25, other arithmetic, backward(): accum = accum.at[a:a + rows, b:b + cols].add(back[3 * a + b])  7.39 us
  transfers between devices with their start and end apart: 7, of which 7 were waited for; matrix products, arithmetic and copies ran while one was open for 10% of the time, Pallas kernels for 0%

commit v1 on v0

--- a/solution.py
+++ b/solution.py
@@ -80,7 +80,29 @@
     here = lax.axis_index("replica")
     share_rows = width // replicas
     mean_delta = lax.psum(delta.astype(jnp.bfloat16), "replica").astype(jnp.float32) / replicas
-    mom_whole = lax.all_gather(momentum[0], "replica", axis=1, tiled=True)
+    ways, here_2, step_2 = (
+        lax.axis_size("replica"),
+        lax.axis_index("replica"),
+        momentum[0].shape[1],
+    )
+    shape = [n * ways if d == 1 else n for d, n in enumerate(momentum[0].shape)]
+    full = lax.dynamic_update_slice_in_dim(
+        jnp.zeros(shape, momentum[0].dtype), momentum[0], here_2 * step_2, axis=1
+    )
+    going_up = going_down = momentum[0]
+    for far in range(1, ways // 2 + 1):
+        going_up = lax.ppermute(going_up, "replica", [(d, (d + 1) % ways) for d in range(ways)])
+        full = lax.dynamic_update_slice_in_dim(
+            full, going_up, (here_2 - far) % ways * step_2, axis=1
+        )
+        if 2 * far < ways:
+            going_down = lax.ppermute(
+                going_down, "replica", [(d, (d - 1) % ways) for d in range(ways)]
+            )
+            full = lax.dynamic_update_slice_in_dim(
+                full, going_down, (here_2 + far) % ways * step_2, axis=1
+            )
+    mom_whole = full
     mom_next = 0.9 * mom_whole + mean_delta
     new_params = params[0] - 0.7 * (mean_delta + 0.9 * mom_next)
     new_momentum = lax.dynamic_slice_in_dim(mom_next, here * share_rows, share_rows, 1)

time: 209 us -> 196 us (0.938)
  waiting for transfers between devices: 73.4 us -> 46.4 us
  local copies, waits for them, and re-layouts: 35.3 us -> 44.7 us
  starting transfers between devices: 6.54 us -> 11.5 us
    all_gather x1 -> x0, waiting for transfers between devices: 25.8 us -> none  [per_device(): mom_whole = lax.all_gather(momentum[0], 'replica', axis=1, tiled=True)]
    psum x1, waiting for transfers between devices: 37.8 us -> 28.5 us  [per_device(): lax.psum(delta.astype(jnp.bfloat16), 'replica').astype(jnp.float32)]
    ppermute x0 -> x3, waiting for transfers between devices: none -> 8.71 us  [the longest x2 8.71 us: per_device(): lax.ppermute(going_up, 'replica', [(d, (d + 1) % ways) for d in range(way...]
    dynamic_update_slice x0 -> x4, local copies, waits for them, and re-layouts: none -> 6.7 us  [the longest x2 3.88 us: per_device(): lax.dynamic_update_slice_in_dim(full, going_up, (here_2 - far) % ways * s...]
    ppermute x0 -> x3, starting transfers between devices: none -> 5.01 us  [the longest x2 3.01 us: per_device(): lax.ppermute(going_up, 'replica', [(d, (d + 1) % ways) for d in range(way...]
    another operation x15 -> x16, local copies, waits for them, and re-layouts: 6.44 us -> 8.13 us
  transfers between devices with their start and end apart: 7 -> 9, of which waited for: 7 -> 7; matrix products, arithmetic and copies ran while one was open for 10% -> 56% of each run, Pallas kernels for 0% -> 0%
where the time goes in v1:
time: 196 us; the launch traced here: 195 us
  waiting for transfers between devices  46.4 us (24%)
  local copies, waits for them, and re-layouts  44.7 us (23%)
  other arithmetic  40.6 us (21%)
  matrix products  29.7 us (15%)
  between operations  14.1 us (7%)
  starting transfers between devices  11.5 us (6%)
  loops' own time  7.98 us (4%)
    psum x1, waiting for transfers between devices, per_device(): lax.psum(delta.astype(jnp.bfloat16), 'replica').astype(jnp.float32)  28.5 us
    scatter-add x35, local copies, waits for them, and re-layouts, backward(): accum = accum.at[a:a + rows, b:b + cols].add(back[3 * a + b])  22.8 us
    dot_general x5, matrix products, backward(): jnp.einsum('krcd,rce->kde', taps, local, preferred_element_type=jnp.float32)  20.2 us
    another operation x15, other arithmetic  13.9 us
    ppermute x5, waiting for transfers between devices, from_behind(): return lax.ppermute(x, axis, pairs)  9.15 us
    ppermute x2, waiting for transfers between devices, per_device(): lax.ppermute(going_up, 'replica', [(d, (d + 1) % ways) for d in range(way...  8.71 us
    another operation x16, local copies, waits for them, and re-layouts  8.13 us
    another operation x1, loops' own time, per_device(): unused, grad_total = lax.fori_loop(0, sections + micro - 1, tick, start)  7.98 us
  transfers between devices with their start and end apart: 9, of which 7 were waited for; matrix products, arithmetic and copies ran while one was open for 56% of the time, Pallas kernels for 0%

profile of v1, /device:TPU:0, one launch (start us, length us, event | category | flops | bytes accessed | tf_op | source)
XLA Modules:
  0.0 195.0 jit_solution(11019723705923721432)
XLA Ops:
  7.7 2.0 %collective-permute-start.2 = (f32[9,64,256]{2,1,0:T(8,128)}, f32[9,64,256]{2,1,0:T(8,128)}, u32[]{:S(2)}, u32[]{:S(2)}) collective-permute-start(f32[9,64,256]{2,1,0:T(8,128)} %bitcast.241), channel_id=1, source_target_pairs={{0,3},{1,0},{2,1},{3,2},{4,7},{5,4},{6,5},{7,6},{8,11},{9,8},{10,9... | collective-permute-start | bytes 1769480 | tf_op jit(solution)/shard_map/ppermute | solution.py:99
  10.7 1.8 bitcast_convert_fusion
  12.5 8.7 %collective-permute-done.1 = f32[9,64,256]{2,1,0:T(8,128)} collective-permute-done((f32[9,64,256]{2,1,0:T(8,128)}, f32[9,64,256]{2,1,0:T(8,128)}, u32[]{:S(2)}, u32[]{:S(2)}) %collective-permute-start.1) | collective-permute-done | bytes 589856 | tf_op jit(solution)/shard_map/ppermute | solution.py:94
  21.2 2.5 %collective-permute-start.3 = (f32[9,64,256]{2,1,0:T(8,128)}, f32[9,64,256]{2,1,0:T(8,128)}, u32[]{:S(2)}, u32[]{:S(2)}) collective-permute-start(f32[9,64,256]{2,1,0:T(8,128)} %collective-permute-done.1), channel_id=1, source_target_pairs={{0,1},{1,2},{2,3},{3,0},{4,5},{5,6},{6,7},{7,4},{8,9},{9,10},{10,1... | collective-permute-start | bytes 1769480 | tf_op jit(solution)/shard_map/ppermute | solution.py:94
  23.8 119.3 %while.28 = (s32[]{:T(128)}, bf16[16,16,256]{2,1,0:T(8,128)(2,1)S(1)}, f32[9,256,256]{2,1,0:T(8,128)}, pred[]{:T(512)}, s32[]{:T(128)}, /*index=5*/bf16[2,16,16,...) while((s32[]{:T(128)}, ...), condition=%wide.region_3.4_spmd.clone, body=%wide.region_0.3_spmd.clone.sunk | while | flops 910100672 | bytes 44110644 | solution.py:75
  31.6 1.6 scatter-add.71
  34.0 2.0 %add_select_fusion.2 = f32[16,16,256]{2,1,0:T(8,128)S(1)} fusion(f32[9,16,16,256]{3,2,1,0:T(8,128)S(1)} %convolution_bitcast_fusion.2, f32[18,18,256]{2,1,0:T(8,128)S(1)} %scatter-add.71, s32[]{:T(128)} %bitcast.237, s32[]{:T(128)} %bitcast.238, pred[]{:T(512)} %and_reduce_fusion.2), kind=kLoop, calls=%fused_computation.14.clone.1 | loop fusion | flops 131072 | bytes 786441 | tf_op jit(solution)/shard_map/select.85
  36.0 1.6 scatter-add.72
  41.8 3.4 %fusion.113 = f32[9,256,256]{2,1,0:T(8,128)} fusion(f32[9,256,256]{2,1,0:T(8,128)} %get-tuple-element.608, bf16[9,16,16,256]{3,2,0,1:T(8,128)(2,1)} %copy-done.8, pred[]{:T(512)S(6)} %compare.183, pred[]{:T(512)S(6)} %and.129, bf16[16,16,256]{2,1,0:T(8,128)(2,1)} %copy-done.6), kind=kOutput, calls=%fused_computation.2.clone.1 | convolution fusion | flops 304349184 | bytes 6029314 | tf_op jit(solution)/shard_map/while/body/eval_jaxpr/krcd,rce->kde/dot_general | solution.py:32
  45.2 2.1 %collective-permute-done = bf16[16,16,256]{2,1,0:T(8,128)(2,1)S(1)} collective-permute-done((bf16[16,16,256]{2,1,0:T(8,128)(2,1)S(1)}, bf16[16,16,256]{2,1,0:T(8,128)(2,1)S(1)}, u32[]{:S(2)}, u32[]{:S(2)}) %collective-permute-start) | collective-permute-done | bytes 131104 | tf_op jit(solution)/shard_map/while/body/eval_jaxpr/ppermute | solution.py:13
  57.5 2.0 %add_select_fusion.2 = f32[16,16,256]{2,1,0:T(8,128)S(1)} fusion(f32[9,16,16,256]{3,2,1,0:T(8,128)S(1)} %convolution_bitcast_fusion.2, f32[18,18,256]{2,1,0:T(8,128)S(1)} %scatter-add.71, s32[]{:T(128)} %bitcast.237, s32[]{:T(128)} %bitcast.238, pred[]{:T(512)} %and_reduce_fusion.2), kind=kLoop, calls=%fused_computation.14.clone.1 | loop fusion | flops 131072 | bytes 786441 | tf_op jit(solution)/shard_map/select.85
  59.5 1.6 scatter-add.72
  65.3 4.2 %fusion.113 = f32[9,256,256]{2,1,0:T(8,128)} fusion(f32[9,256,256]{2,1,0:T(8,128)} %get-tuple-element.608, bf16[9,16,16,256]{3,2,0,1:T(8,128)(2,1)} %copy-done.8, pred[]{:T(512)S(6)} %compare.183, pred[]{:T(512)S(6)} %and.129, bf16[16,16,256]{2,1,0:T(8,128)(2,1)} %copy-done.6), kind=kOutput, calls=%fused_computation.2.clone.1 | convolution fusion | flops 304349184 | bytes 6029314 | tf_op jit(solution)/shard_map/while/body/eval_jaxpr/krcd,rce->kde/dot_general | solution.py:32
  69.5 2.5 %collective-permute-done = bf16[16,16,256]{2,1,0:T(8,128)(2,1)S(1)} collective-permute-done((bf16[16,16,256]{2,1,0:T(8,128)(2,1)S(1)}, bf16[16,16,256]{2,1,0:T(8,128)(2,1)S(1)}, u32[]{:S(2)}, u32[]{:S(2)}) %collective-permute-start) | collective-permute-done | bytes 131104 | tf_op jit(solution)/shard_map/while/body/eval_jaxpr/ppermute | solution.py:13
  82.2 2.0 %add_select_fusion.2 = f32[16,16,256]{2,1,0:T(8,128)S(1)} fusion(f32[9,16,16,256]{3,2,1,0:T(8,128)S(1)} %convolution_bitcast_fusion.2, f32[18,18,256]{2,1,0:T(8,128)S(1)} %scatter-add.71, s32[]{:T(128)} %bitcast.237, s32[]{:T(128)} %bitcast.238, pred[]{:T(512)} %and_reduce_fusion.2), kind=kLoop, calls=%fused_computation.14.clone.1 | loop fusion | flops 131072 | bytes 786441 | tf_op jit(solution)/shard_map/select.85
  84.2 1.6 scatter-add.72
  89.9 4.2 %fusion.113 = f32[9,256,256]{2,1,0:T(8,128)} fusion(f32[9,256,256]{2,1,0:T(8,128)} %get-tuple-element.608, bf16[9,16,16,256]{3,2,0,1:T(8,128)(2,1)} %copy-done.8, pred[]{:T(512)S(6)} %compare.183, pred[]{:T(512)S(6)} %and.129, bf16[16,16,256]{2,1,0:T(8,128)(2,1)} %copy-done.6), kind=kOutput, calls=%fused_computation.2.clone.1 | convolution fusion | flops 304349184 | bytes 6029314 | tf_op jit(solution)/shard_map/while/body/eval_jaxpr/krcd,rce->kde/dot_general | solution.py:32
  94.1 1.9 collective-permute-done
  103.9 1.6 scatter-add.71
  106.2 2.0 %add_select_fusion.2 = f32[16,16,256]{2,1,0:T(8,128)S(1)} fusion(f32[9,16,16,256]{3,2,1,0:T(8,128)S(1)} %convolution_bitcast_fusion.2, f32[18,18,256]{2,1,0:T(8,128)S(1)} %scatter-add.71, s32[]{:T(128)} %bitcast.237, s32[]{:T(128)} %bitcast.238, pred[]{:T(512)} %and_reduce_fusion.2), kind=kLoop, calls=%fused_computation.14.clone.1 | loop fusion | flops 131072 | bytes 786441 | tf_op jit(solution)/shard_map/select.85
  108.2 1.6 scatter-add.72
  114.0 4.2 %fusion.113 = f32[9,256,256]{2,1,0:T(8,128)} fusion(f32[9,256,256]{2,1,0:T(8,128)} %get-tuple-element.608, bf16[9,16,16,256]{3,2,0,1:T(8,128)(2,1)} %copy-done.8, pred[]{:T(512)S(6)} %compare.183, pred[]{:T(512)S(6)} %and.129, bf16[16,16,256]{2,1,0:T(8,128)(2,1)} %copy-done.6), kind=kOutput, calls=%fused_computation.2.clone.1 | convolution fusion | flops 304349184 | bytes 6029314 | tf_op jit(solution)/shard_map/while/body/eval_jaxpr/krcd,rce->kde/dot_general | solution.py:32
  129.7 2.0 %add_select_fusion.2 = f32[16,16,256]{2,1,0:T(8,128)S(1)} fusion(f32[9,16,16,256]{3,2,1,0:T(8,128)S(1)} %convolution_bitcast_fusion.2, f32[18,18,256]{2,1,0:T(8,128)S(1)} %scatter-add.71, s32[]{:T(128)} %bitcast.237, s32[]{:T(128)} %bitcast.238, pred[]{:T(512)} %and_reduce_fusion.2), kind=kLoop, calls=%fused_computation.14.clone.1 | loop fusion | flops 131072 | bytes 786441 | tf_op jit(solution)/shard_map/select.85
  131.7 1.6 scatter-add.72
  137.5 4.2 %fusion.113 = f32[9,256,256]{2,1,0:T(8,128)} fusion(f32[9,256,256]{2,1,0:T(8,128)} %get-tuple-element.608, bf16[9,16,16,256]{3,2,0,1:T(8,128)(2,1)} %copy-done.8, pred[]{:T(512)S(6)} %compare.183, pred[]{:T(512)S(6)} %and.129, bf16[16,16,256]{2,1,0:T(8,128)(2,1)} %copy-done.6), kind=kOutput, calls=%fused_computation.2.clone.1 | convolution fusion | flops 304349184 | bytes 6029314 | tf_op jit(solution)/shard_map/while/body/eval_jaxpr/krcd,rce->kde/dot_general | solution.py:32
  143.0 3.3 %fusion.56 = bf16[9,256,256]{2,1,0:T(8,128)(2,1)} fusion(f32[9,256,256]{2,1,0:T(8,128)} %get-tuple-element.472, bf16[1,1,9,256,256]{4,3,2,1,0:T(8,128)(2,1)} %param.29), kind=kLoop, calls=%fused_computation.72 | loop fusion | flops 2359296 | bytes 4718592 | tf_op jit(solution)/shard_map/convert_element_type | solution.py:76
  146.4 1.6 broadcast.430
  148.9 2.0 %constant_dynamic-update-slice_fusion.2 = f32[9,256,256]{2,1,0:T(8,128)} fusion(f32[9,256,256]{2,1,0:T(8,128)} %constant_dynamic-update-slice_fusion.3, f32[9,64,256]{2,1,0:T(8,128)} %collective-permute-done.1, s32[]{:T(128)S(6)} %select_n.85), kind=kLoop, calls=%fused_computation.82 | loop fusion | bytes 1179652 | tf_op jit(solution)/shard_map/dynamic_update_slice | solution.py:95
  150.9 1.9 constant_dynamic-update-slice_fusion.1
  152.8 1.9 constant_dynamic-update-slice_fusion
  154.8 28.5 %all-reduce.4.cloned.1.call-done = bf16[9,256,256]{2,1,0:T(8,128)(2,1)} async-done(((bf16[9,256,256]{2,1,0:T(8,128)(2,1)}), bf16[9,256,256]{2,1,0:T(8,128)(2,1)}) %all-reduce.4.cloned.1.call-update) | async-done | bytes 1179664 | tf_op jit(solution)/shard_map/psum | solution.py:82
  183.3 4.0 %multiply_add_fusion = (f32[9,256,256]{2,1,0:T(8,128)S(1)}, f32[1,9,256,256]{3,2,1,0:T(8,128)}) fusion(f32[9,256,256]{2,1,0:T(8,128)} %constant_dynamic-update-slice_fusion, bf16[9,256,256]{2,1,0:T(8,128)(2,1)} %all-reduce.4.cloned.1.call-done, f32[1,9,256,256]{3,2,1,0:T(8,128)S(1)} %copy-done.4), kind=kLoop, calls=%fused_computation.76 | loop fusion | flops 4718592 | bytes 10616832 | tf_op jit(solution)/shard_map/add | solution.py:106
  (268 shorter events, 66.8 us)
Async XLA Ops:
  7.2 16.6 %copy-start.9 = (s32[3]{0:T(128)S(1)}, s32[3]{0:T(128)}, u32[]{:S(2)}) copy-start(s32[3]{0:T(128)} %constant.622.clone.2) | copy-start | bytes 40
  7.2 16.6 %copy-start.10 = (s32[1,2]{1,0:T(1,128)S(1)}, s32[1,2]{1,0:T(1,128)}, u32[]{:S(2)}) copy-start(s32[1,2]{1,0:T(1,128)} %param.28) | copy-start | bytes 28
  7.2 176.1 %all-reduce.4.cloned.1.call-start = ((), (), s32[]{:S(2)}) async-start(), calls=%async_computation | async-start | bytes 2359296 | tf_op jit(solution)/shard_map/psum | solution.py:82
  7.2 14.0 %collective-permute-start.1 = (f32[9,64,256]{2,1,0:T(8,128)}, f32[9,64,256]{2,1,0:T(8,128)}, u32[]{:S(2)}, u32[]{:S(2)}) collective-permute-start(f32[9,64,256]{2,1,0:T(8,128)} %bitcast.240), channel_id=1, source_target_pairs={{0,1},{1,2},{2,3},{3,0},{4,5},{5,6},{6,7},{7,4},{8,9},{9,10},{10,1... | collective-permute-start | bytes 1769480 | tf_op jit(solution)/shard_map/ppermute | solution.py:94
  7.7 143.2 %collective-permute-start.2 = (f32[9,64,256]{2,1,0:T(8,128)}, f32[9,64,256]{2,1,0:T(8,128)}, u32[]{:S(2)}, u32[]{:S(2)}) collective-permute-start(f32[9,64,256]{2,1,0:T(8,128)} %bitcast.241), channel_id=1, source_target_pairs={{0,3},{1,0},{2,1},{3,2},{4,7},{5,4},{6,5},{7,6},{8,11},{9,8},{10,9... | collective-permute-start | bytes 1769480 | tf_op jit(solution)/shard_map/ppermute | solution.py:99
  21.2 131.6 %collective-permute-start.3 = (f32[9,64,256]{2,1,0:T(8,128)}, f32[9,64,256]{2,1,0:T(8,128)}, u32[]{:S(2)}, u32[]{:S(2)}) collective-permute-start(f32[9,64,256]{2,1,0:T(8,128)} %collective-permute-done.1), channel_id=1, source_target_pairs={{0,1},{1,2},{2,3},{3,0},{4,5},{5,6},{6,7},{7,4},{8,9},{9,10},{10,1... | collective-permute-start | bytes 1769480 | tf_op jit(solution)/shard_map/ppermute | solution.py:94
  23.8 3.2 %copy-start.2 = (bf16[2,16,16,256]{3,2,0,1:T(8,128)(2,1)}, bf16[2,16,16,256]{3,2,0,1:T(8,128)(2,1)S(1)}, u32[]{:S(2)}) copy-start(bf16[2,16,16,256]{3,2,0,1:T(8,128)(2,1)S(1)} %get-tuple-element.629) | copy-start | bytes 786436 | tf_op jit(solution)/shard_map/while
  23.8 3.2 %copy-start.5 = (bf16[16,16,256]{2,1,0:T(8,128)(2,1)}, bf16[16,16,256]{2,1,0:T(8,128)(2,1)S(1)}, u32[]{:S(2)}) copy-start(bf16[16,16,256]{2,1,0:T(8,128)(2,1)S(1)} %get-tuple-element.607) | copy-start | bytes 393220 | tf_op jit(solution)/shard_map/while
  23.8 4.6 %copy-start = (bf16[9,256,256]{2,1,0:T(8,128)(2,1)}, bf16[9,256,256]{2,1,0:T(8,128)(2,1)S(1)}, u32[]{:S(2)}) copy-start(bf16[9,256,256]{2,1,0:T(8,128)(2,1)S(1)} %get-tuple-element.630) | copy-start | bytes 3538948 | tf_op jit(solution)/shard_map/while
  40.4 6.9 %collective-permute-start = (bf16[16,16,256]{2,1,0:T(8,128)(2,1)S(1)}, bf16[16,16,256]{2,1,0:T(8,128)(2,1)S(1)}, u32[]{:S(2)}, u32[]{:S(2)}) collective-permute-start(bf16[16,16,256]{2,1,0:T(8,128)(2,1)S(1)} %fusion.112), channel_id=1, source_target_pairs={{4,0},{8,4},{12,8},{5,1},{9,5},{13,9},{6,2},{10,6},{14,10},{7,3},{... | collective-permute-start | bytes 393224 | tf_op jit(solution)/shard_map/while/body/eval_jaxpr/ppermute | solution.py:13
  41.7 5.6 %copy-start.1 = (bf16[9,256,256]{2,1,0:T(8,128)(2,1)S(1)}, bf16[9,256,256]{2,1,0:T(8,128)(2,1)}, u32[]{:S(2)}) copy-start(bf16[9,256,256]{2,1,0:T(8,128)(2,1)} %copy-done) | copy-start | bytes 3538948 | tf_op jit(solution)/shard_map/while
  41.8 5.5 %copy-start.3 = (bf16[2,16,16,256]{3,2,0,1:T(8,128)(2,1)S(1)}, bf16[2,16,16,256]{3,2,0,1:T(8,128)(2,1)}, u32[]{:S(2)}) copy-start(bf16[2,16,16,256]{3,2,0,1:T(8,128)(2,1)} %copy-done.2) | copy-start | bytes 786436 | tf_op jit(solution)/shard_map/while
  47.3 3.2 %copy-start.5 = (bf16[16,16,256]{2,1,0:T(8,128)(2,1)}, bf16[16,16,256]{2,1,0:T(8,128)(2,1)S(1)}, u32[]{:S(2)}) copy-start(bf16[16,16,256]{2,1,0:T(8,128)(2,1)S(1)} %get-tuple-element.607) | copy-start | bytes 393220 | tf_op jit(solution)/shard_map/while
  47.3 4.6 %copy-start = (bf16[9,256,256]{2,1,0:T(8,128)(2,1)}, bf16[9,256,256]{2,1,0:T(8,128)(2,1)S(1)}, u32[]{:S(2)}) copy-start(bf16[9,256,256]{2,1,0:T(8,128)(2,1)S(1)} %get-tuple-element.630) | copy-start | bytes 3538948 | tf_op jit(solution)/shard_map/while
  63.9 8.0 %collective-permute-start = (bf16[16,16,256]{2,1,0:T(8,128)(2,1)S(1)}, bf16[16,16,256]{2,1,0:T(8,128)(2,1)S(1)}, u32[]{:S(2)}, u32[]{:S(2)}) collective-permute-start(bf16[16,16,256]{2,1,0:T(8,128)(2,1)S(1)} %fusion.112), channel_id=1, source_target_pairs={{4,0},{8,4},{12,8},{5,1},{9,5},{13,9},{6,2},{10,6},{14,10},{7,3},{... | collective-permute-start | bytes 393224 | tf_op jit(solution)/shard_map/while/body/eval_jaxpr/ppermute | solution.py:13
  65.3 6.7 %copy-start.1 = (bf16[9,256,256]{2,1,0:T(8,128)(2,1)S(1)}, bf16[9,256,256]{2,1,0:T(8,128)(2,1)}, u32[]{:S(2)}) copy-start(bf16[9,256,256]{2,1,0:T(8,128)(2,1)} %copy-done) | copy-start | bytes 3538948 | tf_op jit(solution)/shard_map/while
  65.3 6.7 %copy-start.3 = (bf16[2,16,16,256]{3,2,0,1:T(8,128)(2,1)S(1)}, bf16[2,16,16,256]{3,2,0,1:T(8,128)(2,1)}, u32[]{:S(2)}) copy-start(bf16[2,16,16,256]{3,2,0,1:T(8,128)(2,1)} %copy-done.2) | copy-start | bytes 786436 | tf_op jit(solution)/shard_map/while
  72.0 3.2 %copy-start.5 = (bf16[16,16,256]{2,1,0:T(8,128)(2,1)}, bf16[16,16,256]{2,1,0:T(8,128)(2,1)S(1)}, u32[]{:S(2)}) copy-start(bf16[16,16,256]{2,1,0:T(8,128)(2,1)S(1)} %get-tuple-element.607) | copy-start | bytes 393220 | tf_op jit(solution)/shard_map/while
  72.0 4.6 %copy-start = (bf16[9,256,256]{2,1,0:T(8,128)(2,1)}, bf16[9,256,256]{2,1,0:T(8,128)(2,1)S(1)}, u32[]{:S(2)}) copy-start(bf16[9,256,256]{2,1,0:T(8,128)(2,1)S(1)} %get-tuple-element.630) | copy-start | bytes 3538948 | tf_op jit(solution)/shard_map/while
  88.6 7.4 %collective-permute-start = (bf16[16,16,256]{2,1,0:T(8,128)(2,1)S(1)}, bf16[16,16,256]{2,1,0:T(8,128)(2,1)S(1)}, u32[]{:S(2)}, u32[]{:S(2)}) collective-permute-start(bf16[16,16,256]{2,1,0:T(8,128)(2,1)S(1)} %fusion.112), channel_id=1, source_target_pairs={{4,0},{8,4},{12,8},{5,1},{9,5},{13,9},{6,2},{10,6},{14,10},{7,3},{... | collective-permute-start | bytes 393224 | tf_op jit(solution)/shard_map/while/body/eval_jaxpr/ppermute | solution.py:13
  89.9 6.1 %copy-start.1 = (bf16[9,256,256]{2,1,0:T(8,128)(2,1)S(1)}, bf16[9,256,256]{2,1,0:T(8,128)(2,1)}, u32[]{:S(2)}) copy-start(bf16[9,256,256]{2,1,0:T(8,128)(2,1)} %copy-done) | copy-start | bytes 3538948 | tf_op jit(solution)/shard_map/while
  89.9 6.1 %copy-start.3 = (bf16[2,16,16,256]{3,2,0,1:T(8,128)(2,1)S(1)}, bf16[2,16,16,256]{3,2,0,1:T(8,128)(2,1)}, u32[]{:S(2)}) copy-start(bf16[2,16,16,256]{3,2,0,1:T(8,128)(2,1)} %copy-done.2) | copy-start | bytes 786436 | tf_op jit(solution)/shard_map/while
  96.0 4.6 %copy-start = (bf16[9,256,256]{2,1,0:T(8,128)(2,1)}, bf16[9,256,256]{2,1,0:T(8,128)(2,1)S(1)}, u32[]{:S(2)}) copy-start(bf16[9,256,256]{2,1,0:T(8,128)(2,1)S(1)} %get-tuple-element.630) | copy-start | bytes 3538948 | tf_op jit(solution)/shard_map/while
  112.7 6.9 %collective-permute-start = (bf16[16,16,256]{2,1,0:T(8,128)(2,1)S(1)}, bf16[16,16,256]{2,1,0:T(8,128)(2,1)S(1)}, u32[]{:S(2)}, u32[]{:S(2)}) collective-permute-start(bf16[16,16,256]{2,1,0:T(8,128)(2,1)S(1)} %fusion.112), channel_id=1, source_target_pairs={{4,0},{8,4},{12,8},{5,1},{9,5},{13,9},{6,2},{10,6},{14,10},{7,3},{... | collective-permute-start | bytes 393224 | tf_op jit(solution)/shard_map/while/body/eval_jaxpr/ppermute | solution.py:13
  114.0 5.6 %copy-start.1 = (bf16[9,256,256]{2,1,0:T(8,128)(2,1)S(1)}, bf16[9,256,256]{2,1,0:T(8,128)(2,1)}, u32[]{:S(2)}) copy-start(bf16[9,256,256]{2,1,0:T(8,128)(2,1)} %copy-done) | copy-start | bytes 3538948 | tf_op jit(solution)/shard_map/while
  114.0 5.5 %copy-start.3 = (bf16[2,16,16,256]{3,2,0,1:T(8,128)(2,1)S(1)}, bf16[2,16,16,256]{3,2,0,1:T(8,128)(2,1)}, u32[]{:S(2)}) copy-start(bf16[2,16,16,256]{3,2,0,1:T(8,128)(2,1)} %copy-done.2) | copy-start | bytes 786436 | tf_op jit(solution)/shard_map/while
  119.5 3.2 %copy-start.5 = (bf16[16,16,256]{2,1,0:T(8,128)(2,1)}, bf16[16,16,256]{2,1,0:T(8,128)(2,1)S(1)}, u32[]{:S(2)}) copy-start(bf16[16,16,256]{2,1,0:T(8,128)(2,1)S(1)} %get-tuple-element.607) | copy-start | bytes 393220 | tf_op jit(solution)/shard_map/while
  119.5 4.6 %copy-start = (bf16[9,256,256]{2,1,0:T(8,128)(2,1)}, bf16[9,256,256]{2,1,0:T(8,128)(2,1)S(1)}, u32[]{:S(2)}) copy-start(bf16[9,256,256]{2,1,0:T(8,128)(2,1)S(1)} %get-tuple-element.630) | copy-start | bytes 3538948 | tf_op jit(solution)/shard_map/while
  136.2 6.9 %collective-permute-start = (bf16[16,16,256]{2,1,0:T(8,128)(2,1)S(1)}, bf16[16,16,256]{2,1,0:T(8,128)(2,1)S(1)}, u32[]{:S(2)}, u32[]{:S(2)}) collective-permute-start(bf16[16,16,256]{2,1,0:T(8,128)(2,1)S(1)} %fusion.112), channel_id=1, source_target_pairs={{4,0},{8,4},{12,8},{5,1},{9,5},{13,9},{6,2},{10,6},{14,10},{7,3},{... | collective-permute-start | bytes 393224 | tf_op jit(solution)/shard_map/while/body/eval_jaxpr/ppermute | solution.py:13
  137.5 5.6 %copy-start.1 = (bf16[9,256,256]{2,1,0:T(8,128)(2,1)S(1)}, bf16[9,256,256]{2,1,0:T(8,128)(2,1)}, u32[]{:S(2)}) copy-start(bf16[9,256,256]{2,1,0:T(8,128)(2,1)} %copy-done) | copy-start | bytes 3538948 | tf_op jit(solution)/shard_map/while
  137.5 5.5 %copy-start.3 = (bf16[2,16,16,256]{3,2,0,1:T(8,128)(2,1)S(1)}, bf16[2,16,16,256]{3,2,0,1:T(8,128)(2,1)}, u32[]{:S(2)}) copy-start(bf16[2,16,16,256]{3,2,0,1:T(8,128)(2,1)} %copy-done.2) | copy-start | bytes 786436 | tf_op jit(solution)/shard_map/while
  148.0 35.2 %copy-start.4 = (f32[1,9,256,256]{3,2,1,0:T(8,128)S(1)}, f32[1,9,256,256]{3,2,1,0:T(8,128)}, u32[]{:S(2)}) copy-start(f32[1,9,256,256]{3,2,1,0:T(8,128)} %param.30) | copy-start | bytes 7077892
  (16 other events, 37.6 us)
Sparse Core Ops, SparseCore 0:
  146.5 36.7 all-reduce.3
